TPU v7x, 512 devices: a whole 4x4x16 slice. The times are simulated.
512 devices in a mesh: track: 8 (over y, core), pix: 64 (over z, x).
Axes of the slice: x: 4, y: 4, z: 16, core: 2. Of those that a mesh axis runs over, the one named last changes fastest.
Arguments:
- phases: bfloat16 [8, 256, 524288], P('track', 'pix'), may hold values from -15 to 15
- coherent: int32 [8, 256, 4096], P('track', 'pix'), may hold values 0 or 1
- pairs: int32 [8, 256, 2], P('track'), may hold values from 0 to 199, as said below
- res_index: int32 [8, 4, 524288], P('track', None, 'pix'), may hold values from -128 to 128, as said below
- res_weight: float32 [8, 4, 524288], P('track', None, 'pix'), may hold values from 0.05 to 1
- coverage: int32 [8, 512, 8], P('track', 'pix'), may hold values 0 or 1
- los: float32 [8, 3], replicated
- north: float32 [512, 1024], P('pix'), may hold values from -6 to 6
Outputs:
- east_up: float32 [2, 512, 1024], P(None, 'pix', 'track')
- strain: float32 [3, 512, 1024], P(None, 'pix', 'track')
Inputs may be any that keep to these rules, and one draw needn't show every extreme that they name: `pairs`: each row holds an earlier epoch and a strictly later one. `res_index`: cell index plus offset lies within 0 to 524287.
All inputs are finite; a program needn't handle non-finite values. No bound on the sum of `coherent` or of `coverage` on one device may be relied on, other than what follows from the above.
Results may differ from a plain program's by a relative error of at most 0.0031.
Values may be sent and summed in bfloat16 or wider, within the bound.
A program may use at most 128 MiB of HBM per device.

v0:
```python
import jax
import jax.numpy as jnp
from jax import lax
from jax.sharding import PartitionSpec as P

IFGS = 256
EPOCHS = 200
GRD = 8
GCOLS = 1024
HALO = 128
CTILE = 128


prior_var = 0.1
ridge_term = 0.5


def with_halo(shard, sides, width):
    for axis, dim in sides:
        size, length = (lax.axis_size(axis), shard.shape[dim])
        up = [(i, (i + 1) % size) for i in range(size - 1)]
        down = [(j, i) for i, j in up]
        last = lax.slice_in_dim(shard, length - width, length, axis=dim)
        initial = lax.slice_in_dim(shard, 0, width, axis=dim)
        before = lax.ppermute(last, axis, up)
        after = lax.ppermute(initial, axis, down)
        shard = jnp.concatenate([before, shard, after], axis=dim)
    return shard


def setup_track(pair_rows):
    epochs = jnp.arange(EPOCHS, dtype=jnp.int32)
    design = (epochs[None, :] == pair_rows[:, 1:2]).astype(jnp.float32) - (
        epochs[None, :] == pair_rows[:, 0:1]
    ).astype(jnp.float32)
    normal = jnp.dot(
        design.T, design, precision=lax.Precision.HIGHEST, preferred_element_type=jnp.float32
    ) + jnp.eye(EPOCHS, dtype=jnp.float32)
    factor = jnp.linalg.cholesky(normal)
    pseudo = jax.scipy.linalg.cho_solve((factor, True), design.T)
    centred = jnp.arange(EPOCHS).astype(jnp.float32) - (EPOCHS - 1) / 2.0
    slope = centred * (EPOCHS - 1) / jnp.sum(centred * centred)
    return (design.astype(jnp.bfloat16), pseudo.astype(jnp.bfloat16), slope)


def invert_block(stack, design_bf, pseudo_bf, slope):
    series = jnp.dot(pseudo_bf, stack, preferred_element_type=jnp.float32)
    velocity = jnp.dot(
        slope, series, precision=lax.Precision.HIGHEST, preferred_element_type=jnp.float32
    )
    fitted = jnp.dot(design_bf, series.astype(jnp.bfloat16), preferred_element_type=jnp.float32)
    misfit = stack.astype(jnp.float32) - fitted
    variance = jnp.sum(misfit * misfit, axis=0) / IFGS
    return jnp.stack([velocity, variance])


def solve_cells(vals, cover, north_part, los):
    east_c = los[:, 0][:, None, None]
    north_c = los[:, 1][:, None, None]
    up_c = los[:, 2][:, None, None]
    weight = cover / (vals[1] + prior_var)
    target = vals[0] - north_c * north_part[None]
    a11 = jnp.sum(weight * east_c * east_c, axis=0) + ridge_term
    a12 = jnp.sum(weight * east_c * up_c, axis=0)
    a22 = jnp.sum(weight * up_c * up_c, axis=0) + ridge_term
    b1 = jnp.sum(weight * east_c * target, axis=0)
    b2 = jnp.sum(weight * up_c * target, axis=0)
    determ = a11 * a22 - a12 * a12
    return ((a22 * b1 - a12 * b2) / determ, (a11 * b2 - a12 * b1) / determ)


def stencil(padded):
    east_p = padded[0]
    north_p = padded[1]
    exx = (east_p[1:-1, 2:] - east_p[1:-1, :-2]) / 2.0
    eyy = (north_p[2:, 1:-1] - north_p[:-2, 1:-1]) / 2.0
    exy = (east_p[2:, 1:-1] - east_p[:-2, 1:-1] + north_p[1:-1, 2:] - north_p[1:-1, :-2]) / 4.0
    return jnp.stack([exx, eyy, exy])


def widen_cover(cover):
    count, rows_here, tiles = cover.shape
    return jnp.broadcast_to(cover[:, :, :, None], (count, rows_here, tiles, CTILE)).reshape(
        count, rows_here, tiles * CTILE
    )


def per_device(phases, coherent, pairs, res_index, res_weight, coverage, los, north):
    design_bf, pseudo_bf, slope = setup_track(pairs[0])
    local_ifgs = phases.shape[1]
    cells = phases.shape[2]
    parts = lax.axis_size("pix")
    width = cells // parts
    blocks = coherent.shape[2]
    blocked = phases[0].reshape(local_ifgs, blocks, cells // blocks)
    masked = jnp.where(coherent[0][:, :, None] == 1, blocked, jnp.zeros((), jnp.bfloat16))
    masked = masked.reshape(local_ifgs, parts, width)
    fields = invert_block(
        lax.all_to_all(masked, "pix", split_axis=1, concat_axis=0, tiled=True)[:, 0, :],
        design_bf,
        pseudo_bf,
        slope,
    )
    extended = with_halo(fields, (("pix", 1),), HALO)
    position = jnp.arange(width, dtype=jnp.int32)
    local = position[None, :] + res_index[0] + HALO
    picked = jnp.take(extended, local, axis=1)
    weight = res_weight[0]
    grid = jnp.sum(picked * weight[None], axis=1) / jnp.sum(weight, axis=0)
    grid_four = grid.reshape(2, 1, GRD, GCOLS)
    cover_four = coverage.astype(jnp.float32).reshape(1, 1, GRD, coverage.shape[2])
    column_block = lax.axis_index("track")
    span = GCOLS // lax.axis_size("track")
    vals, cover = (
        lax.all_to_all(grid_four, "track", split_axis=3, concat_axis=1, tiled=True),
        lax.all_to_all(cover_four, "track", split_axis=3, concat_axis=1, tiled=True),
    )
    cover_cells = widen_cover(cover[0])
    north_own = lax.dynamic_slice_in_dim(north, column_block * span, span, 1)
    east, up = solve_cells(vals, cover_cells, north_own, los)
    padded = with_halo(jnp.stack([east, north_own]), (("pix", 1), ("track", 2)), 1)
    strain = stencil(padded)
    east_up = jnp.stack([east, up])
    return (east_up, strain)


def solution(mesh):
    in_specs = (
        P("track", "pix", None),
        P("track", "pix", None),
        P("track", None, None),
        P("track", None, "pix"),
        P("track", None, "pix"),
        P("track", "pix", None),
        P(),
        P("pix", None),
    )
    out_specs = (P(None, "pix", "track"), P(None, "pix", "track"))
    return jax.shard_map(
        per_device, mesh=mesh, in_specs=in_specs, out_specs=out_specs, check_vma=False
    )
```

profile of v0, /device:TPU:24, one launch (start us, length us, event | category | flops | bytes accessed | tf_op | source)
XLA Modules:
  0.0 432.6 jit_solution(12200225062863417160)
XLA Ops:
  0.6 0.9 compare_bitcast_fusion
  1.5 7.7 %broadcast_in_dim.40 = pred[4,4096,128]{2,1,0:T(8,128)(4,1)} broadcast(pred[4,4096]{1,0:T(4,128)(4,1)S(1)} %compare_bitcast_fusion), dimensions={0,1} | broadcast | bytes 2113536 | tf_op jit(solution)/shard_map/jit(_where)/broadcast_in_dim | solution.py:96
  9.2 5.3 %broadcast_in_dim.41 = pred[4,64,8192]{2,1,0:T(8,128)(4,1)S(1)} reshape(pred[4,4096,128]{2,1,0:T(8,128)(4,1)} %broadcast_in_dim.40) | data formatting | bytes 4194304 | tf_op jit(solution)/shard_map/jit(_where)/broadcast_in_dim | solution.py:96
  14.5 7.0 %bitcast_select_fusion = bf16[4,64,8192]{2,1,0:T(8,128)(2,1)S(1)} fusion(pred[4,64,8192]{2,1,0:T(8,128)(4,1)S(1)} %broadcast_in_dim.41, bf16[1,4,64,8192]{3,1,2,0:T(4,128)(2,1)} %bitcast.134), kind=kLoop, calls=%fused_computation.4 | loop fusion | flops 2097152 | bytes 10485760 | tf_op jit(solution)/shard_map/jit(_where)/select_n | solution.py:96
  21.6 5.2 %copy.46 = bf16[4,64,8192]{2,0,1:T(4,128)(2,1)} copy(bf16[4,64,8192]{2,1,0:T(8,128)(2,1)S(1)} %bitcast_select_fusion) | data formatting | bytes 8388608 | tf_op jit(solution)/shard_map/jit(_where)/select_n | solution.py:96
  26.8 19.1 %all-to-all-start.1 = ((bf16[4,64,8192]{2,0,1:T(4,128)(2,1)}), bf16[4,64,8192]{2,0,1:T(4,128)(2,1)}, u32[]{:S(2)}, u32[]{:S(2)}) async-start(bf16[4,64,8192]{2,0,1:T(4,128)(2,1)} %copy.46), calls=%async_computation.1 | async-start | bytes 8388608 | tf_op jit(solution)/shard_map/all_to_all | solution.py:99
  46.0 0.7 fusion.6
  46.9 11.7 %cholesky.51 = f32[128,128]{1,0:T(8,128)S(1)} custom-call(f32[128,128]{1,0:T(8,128)S(1)} %cholesky.124), custom_call_target="Cholesky" | custom-call | tf_op jit(solution)/shard_map/jit(cholesky)/cholesky | solution.py:39
  58.6 9.8 %custom-call.18 = f32[1,128,128]{1,2,0:T(8,128)S(1)} custom-call(f32[1,128,128]{2,1,0:T(8,128)S(1)} %get-tuple-element.30), custom_call_target="InvertDiagBlocksLowerTriangular" | custom-call | tf_op jit(solution)/shard_map/jit(cholesky)/cholesky | solution.py:39
  68.9 6.6 %cholesky.110 = f32[72,72]{1,0:T(8,128)S(1)} custom-call(f32[72,72]{1,0:T(8,128)S(1)} %convolution_subtract_fusion.3), custom_call_target="Cholesky" | custom-call | tf_op jit(solution)/shard_map/jit(cholesky)/cholesky | solution.py:39
  75.5 0.6 compare_reduce_fusion
  76.2 0.6 compare_reduce_fusion.1
  78.3 19.7 %custom-call.19 = f32[2,128,128]{1,2,0:T(8,128)S(1)} custom-call(f32[2,128,128]{2,1,0:T(8,128)S(1)} %pad_maximum_fusion), custom_call_target="InvertDiagBlocksLowerTriangular" | custom-call | tf_op jit(solution)/shard_map/jit(_cho_solve)/triangular_solve | solution.py:40
  98.1 0.7 copy.41
  98.8 0.6 multiply_reduce_fusion.6
  99.4 0.7 multiply_divide_fusion
  100.1 0.3 fusion.11
  101.1 0.3 convolution_subtract_fusion.1
  101.4 0.3 convolution_convert_fusion
  101.8 133.9 %all-to-all-done.1 = bf16[4,64,8192]{2,0,1:T(4,128)(2,1)} async-done(((bf16[4,64,8192]{2,0,1:T(4,128)(2,1)}), bf16[4,64,8192]{2,0,1:T(4,128)(2,1)}, u32[]{:S(2)}, u32[]{:S(2)}) %all-to-all-start.1) | async-done | bytes 4194336 | tf_op jit(solution)/shard_map/all_to_all | solution.py:99
  235.7 4.9 %all-to-all-start = ((f32[1,1,8,8]{2,1,0,3:T(1,128)}), f32[1,1,8,8]{2,1,0,3:T(1,128)S(1)}, u32[]{:S(2)}, u32[]{:S(2)}) async-start(f32[1,1,8,8]{2,1,0,3:T(1,128)} %copy.41), calls=%async_computation | async-start | bytes 8192 | tf_op jit(solution)/shard_map/all_to_all | solution.py:116
  240.6 6.9 %squeeze.24 = bf16[256,8192]{1,0:T(8,128)(2,1)} reshape(bf16[64,4,1,8192]{3,1,0,2:T(4,128)(2,1)} %bitcast.18) | data formatting | bytes 8388608 | tf_op jit(solution)/shard_map/squeeze | solution.py:99
  247.5 3.4 fusion.17
  251.0 1.8 fusion.2
  252.8 3.2 fusion.44
  256.0 3.4 collective-permute-start
  259.4 1.3 collective-permute-start.1
  261.0 3.8 collective-permute-done.1
  264.9 2.7 copy.47
  267.6 110.4 %gather_fusion = f32[32768,2]{1,0:T(8,128)} fusion(f32[2,8448]{0,1:T(8,128)} %copy.47, s32[32768]{0:T(1024)S(1)} %broadcast_clamp_fusion), kind=kCustom, calls=%fused_computation | custom fusion | bytes 655360 | tf_op jit(solution)/shard_map/jit(_take)/gather | solution.py:107
  378.0 14.8 %multiply_reduce_fusion = f32[8192,2]{1,0:T(8,128)} fusion(f32[4,8192,2]{2,1,0:T(8,128)} %bitcast.132, f32[4,8192]{1,0:T(4,128)S(1)} %bitcast.136, pred[4,8192]{1,0:T(4,128)(4,1)S(1)} %compare_and_fusion), kind=kLoop, calls=%fused_computation.1 | loop fusion | flops 180224 | bytes 491520 | tf_op jit(solution)/shard_map/reduce_sum | solution.py:109
  392.8 8.4 %copy.49 = f32[2,1,8,1024]{2,0,1,3:T(2,128)S(1)} copy(f32[2,1,8,1024]{0,3,2,1:T(8,128)} %bitcast.133) | data formatting | bytes 131072 | tf_op jit(solution)/shard_map/reduce_sum | solution.py:109
  401.2 0.5 fusion.43
  401.7 2.2 reshape.282
  403.9 4.8 %all-to-all-start.2 = ((f32[8,1,2048]{2,1,0:T(1,128)}), f32[8,1,2048]{2,1,0:T(1,128)S(1)}, u32[]{:S(2)}, u32[]{:S(2)}) async-start(f32[8,1,2048]{2,1,0:T(1,128)} %reshape.282), calls=%async_computation.2 | async-start | bytes 131072 | tf_op jit(solution)/shard_map/all_to_all | solution.py:115
  408.8 3.5 all-to-all-done.2
  412.3 0.5 broadcast.304
  412.8 0.8 reduce.15
  413.6 1.6 reshape.283
  415.2 0.4 copy.50
  415.8 3.4 collective-permute-start.2
  419.2 1.3 collective-permute-start.3
  420.5 0.6 pad_maximum_fusion.5
  421.1 3.6 collective-permute-done.3
  424.8 1.9 collective-permute-start.4
  426.7 3.6 collective-permute-start.5
  430.4 1.4 collective-permute-done.5
  431.9 0.6 pad_maximum_fusion.4
  (60 shorter events, 2.7 us)
Async XLA Ops:
  0.6 260.0 %copy-start = (f32[8,1024]{1,0:T(8,128)S(1)}, f32[8,1024]{1,0:T(8,128)}, u32[]{:S(2)}) copy-start(f32[8,1024]{1,0:T(8,128)} %param.15) | copy-start | bytes 98308
  26.8 19.2 %copy-start.5 = (s32[1,256,2]{1,2,0:T(2,128)S(1)}, s32[1,256,2]{1,2,0:T(2,128)}, u32[]{:S(2)}) copy-start(s32[1,256,2]{1,2,0:T(2,128)} %param.10) | copy-start | bytes 6148
  26.8 71.2 %copy-start.3 = (s32[1,4,8192]{2,1,0:T(4,128)S(1)}, s32[1,4,8192]{2,1,0:T(4,128)}, u32[]{:S(2)}) copy-start(s32[1,4,8192]{2,1,0:T(4,128)} %param.11) | copy-start | bytes 393220
  26.8 71.3 %copy-start.4 = (s32[1,8,8]{2,1,0:T(8,128)S(1)}, s32[1,8,8]{2,1,0:T(8,128)}, u32[]{:S(2)}) copy-start(s32[1,8,8]{2,1,0:T(8,128)} %param.13) | copy-start | bytes 772
  26.8 73.3 %copy-start.6 = (f32[8,3]{0,1:T(4,128)S(1)}, f32[8,3]{0,1:T(4,128)}, u32[]{:S(2)}) copy-start(f32[8,3]{0,1:T(4,128)} %param.14) | copy-start | bytes 292
  26.8 208.9 %all-to-all-start.1 = ((bf16[4,64,8192]{2,0,1:T(4,128)(2,1)}), bf16[4,64,8192]{2,0,1:T(4,128)(2,1)}, u32[]{:S(2)}, u32[]{:S(2)}) async-start(bf16[4,64,8192]{2,0,1:T(4,128)(2,1)} %copy.46), calls=%async_computation.1 | async-start | bytes 8388608 | tf_op jit(solution)/shard_map/all_to_all | solution.py:99
  235.7 168.2 %all-to-all-start = ((f32[1,1,8,8]{2,1,0,3:T(1,128)}), f32[1,1,8,8]{2,1,0,3:T(1,128)S(1)}, u32[]{:S(2)}, u32[]{:S(2)}) async-start(f32[1,1,8,8]{2,1,0,3:T(1,128)} %copy.41), calls=%async_computation | async-start | bytes 8192 | tf_op jit(solution)/shard_map/all_to_all | solution.py:116
  247.5 3.4 copy-start.1
  252.8 7.9 %copy-start.2 = (f32[1,4,8192]{2,1,0:T(4,128)S(1)}, f32[1,4,8192]{2,1,0:T(4,128)}, u32[]{:S(2)}) copy-start(f32[1,4,8192]{2,1,0:T(4,128)} %param.12) | copy-start | bytes 393220
  256.0 5.0 %collective-permute-start = (f32[2,128]{1,0:T(2,128)S(1)}, f32[2,128]{1,0:T(2,128)S(1)}, u32[]{:S(2)}, u32[]{:S(2)}) collective-permute-start(f32[2,128]{1,0:T(2,128)S(1)} %get-tuple-element.27), channel_id=1, source_target_pairs={{0,1},{1,2},{2,3},{3,4},{4,5},{5,6},{6,7},{7,8},{8,9},{9,10},{10,1... | collective-permute-start | bytes 3080 | tf_op jit(solution)/shard_map/ppermute | solution.py:25
  259.4 5.5 %collective-permute-start.1 = (f32[2,128]{1,0:T(2,128)S(1)}, f32[2,128]{1,0:T(2,128)S(1)}, u32[]{:S(2)}, u32[]{:S(2)}) collective-permute-start(f32[2,128]{1,0:T(2,128)S(1)} %get-tuple-element.28), channel_id=1, source_target_pairs={{1,0},{2,1},{3,2},{4,3},{5,4},{6,5},{7,6},{8,7},{9,8},{10,9},{11,1... | collective-permute-start | bytes 3080 | tf_op jit(solution)/shard_map/ppermute | solution.py:26
  403.9 8.4 %all-to-all-start.2 = ((f32[8,1,2048]{2,1,0:T(1,128)}), f32[8,1,2048]{2,1,0:T(1,128)S(1)}, u32[]{:S(2)}, u32[]{:S(2)}) async-start(f32[8,1,2048]{2,1,0:T(1,128)} %reshape.282), calls=%async_computation.2 | async-start | bytes 131072 | tf_op jit(solution)/shard_map/all_to_all | solution.py:115
  415.8 5.3 %collective-permute-start.2 = (f32[2,1,128]{2,1,0:T(1,128)S(1)}, f32[2,1,128]{2,1,0:T(1,128)S(1)}, u32[]{:S(2)}, u32[]{:S(2)}) collective-permute-start(f32[2,1,128]{2,1,0:T(1,128)S(1)} %get-tuple-element.42), channel_id=1, source_target_pairs={{0,1},{1,2},{2,3},{3,4},{4,5},{5,6},{6,7},{7,8},{8,9},{9,10},{10,1... | collective-permute-start | bytes 3080 | tf_op jit(solution)/shard_map/ppermute | solution.py:25
  419.2 5.5 %collective-permute-start.3 = (f32[2,1,128]{2,1,0:T(1,128)S(1)}, f32[2,1,128]{2,1,0:T(1,128)S(1)}, u32[]{:S(2)}, u32[]{:S(2)}) collective-permute-start(f32[2,1,128]{2,1,0:T(1,128)S(1)} %get-tuple-element.43), channel_id=1, source_target_pairs={{1,0},{2,1},{3,2},{4,3},{5,4},{6,5},{7,6},{8,7},{9,8},{10,9},{11,1... | collective-permute-start | bytes 3080 | tf_op jit(solution)/shard_map/ppermute | solution.py:26
  424.8 5.6 %collective-permute-start.4 = (f32[2,10,1]{2,1,0:T(8,128)S(1)}, f32[2,10,1]{2,1,0:T(8,128)S(1)}, u32[]{:S(2)}, u32[]{:S(2)}) collective-permute-start(f32[2,10,1]{2,1,0:T(8,128)S(1)} %get-tuple-element.40), channel_id=1, source_target_pairs={{0,64},{64,128},{128,192},{192,256},{256,320},{320,384},{384,448},... | collective-permute-start | bytes 248 | tf_op jit(solution)/shard_map/ppermute | solution.py:25
  426.7 5.1 %collective-permute-start.5 = (f32[2,10,1]{2,1,0:T(8,128)S(1)}, f32[2,10,1]{2,1,0:T(8,128)S(1)}, u32[]{:S(2)}, u32[]{:S(2)}) collective-permute-start(f32[2,10,1]{2,1,0:T(8,128)S(1)} %get-tuple-element.41), channel_id=1, source_target_pairs={{64,0},{128,64},{192,128},{256,192},{320,256},{384,320},{448,384},... | collective-permute-start | bytes 248 | tf_op jit(solution)/shard_map/ppermute | solution.py:26
where the time goes:
time: 437 us; the launch traced here: 433 us
  local copies, waits for them, and re-layouts  153 us (35%)
  waiting for transfers between devices  146 us (33%)
  other arithmetic  76.5 us (18%)
  starting transfers between devices  43.7 us (10%)
  matrix products  11.1 us (3%)
    all_to_all x1, waiting for transfers between devices, per_device(): lax.all_to_all(masked, 'pix', split_axis=1, concat_axis=0, tiled=True)  134 us
    gather x1, local copies, waits for them, and re-layouts, per_device(): picked = jnp.take(extended, local, axis=1)  110 us
    another operation x7, other arithmetic, setup_track(): factor = jnp.linalg.cholesky(normal)  29.4 us
    another operation x6, other arithmetic, setup_track(): pseudo = jax.scipy.linalg.cho_solve((factor, True), design.T)  19.8 us
    all_to_all x1, starting transfers between devices, per_device(): lax.all_to_all(masked, 'pix', split_axis=1, concat_axis=0, tiled=True)  19.1 us
    reduce_sum x2, other arithmetic, per_device(): grid = jnp.sum(picked * weight[None], axis=1) / jnp.sum(weight, axis=0)  14.8 us
    broadcast_in_dim x2, local copies, waits for them, and re-layouts, per_device(): jnp.where(coherent[0][:, :, None] == 1, blocked, jnp.zeros((), jnp.bfloat...  13 us
    ppermute x3, waiting for transfers between devices, with_halo(): after = lax.ppermute(initial, axis, down)  8.79 us
  transfers between devices with their start and end apart: 9, of which 5 were waited for; matrix products, arithmetic and copies ran while one was open for 48% of the time, Pallas kernels for 0%

commit v1 on v0

v1 whole, which is shorter than its diff:
```python
import jax
import jax.numpy as jnp
from jax import lax
from jax.experimental import pallas as pl
from jax.experimental.pallas import tpu as pltpu
from jax.sharding import PartitionSpec as P

IFGS = 256
EPOCHS = 200
GRD = 8
GCOLS = 1024
LANES = 128
TILES = GCOLS // LANES
PIX = 64
TRACKS = 8
LOCAL = IFGS // PIX
KPAD = 256

prior_var = 0.1
ridge_term = 0.5

MESH = pl.DeviceIdType.MESH
F32 = jnp.float32
BF16 = jnp.bfloat16
HIGHEST = lax.Precision.HIGHEST


def iota(shape, dim):
    return lax.broadcasted_iota(jnp.int32, shape, dim)


def setup(pairs, normal, weights, design):
    epoch = iota((KPAD, IFGS), 0)
    design_t = (epoch == pairs[1:2, :]).astype(F32) - (epoch == pairs[0:1, :]).astype(F32)
    design[...] = design_t.T.astype(BF16)
    gram = lax.dot_general(
        design_t.astype(BF16), design_t.astype(BF16), (((1,), (1,)), ((), ())), preferred_element_type=F32
    )
    normal[...] = gram + (iota((KPAD, KPAD), 0) == iota((KPAD, KPAD), 1)).astype(F32)

    def eliminate(k, carry):
        row = normal[pl.ds(k, 1), :]
        here = iota((1, KPAD), 1) == k
        inverse = 1.0 / jnp.sum(jnp.where(here, row, 0.0), axis=1, keepdims=True)
        scaled = jnp.where(here, inverse, row * inverse)
        block = normal[0:EPOCHS, :]
        at_k = iota((EPOCHS, KPAD), 1) == k
        column = jnp.sum(jnp.where(at_k, block, 0.0), axis=1, keepdims=True)
        normal[0:EPOCHS, :] = jnp.where(at_k, 0.0, block) - column * scaled
        normal[pl.ds(k, 1), :] = scaled
        return carry

    lax.fori_loop(0, EPOCHS, eliminate, 0)
    pseudo = jnp.dot(normal[...], design_t, precision=HIGHEST, preferred_element_type=F32)
    pseudo = jnp.where(iota((KPAD, IFGS), 0) < EPOCHS, pseudo, 0.0).astype(BF16).astype(F32)
    centred = iota((KPAD, 1), 0).astype(F32) - (EPOCHS - 1) / 2.0
    total = EPOCHS * (EPOCHS * EPOCHS - 1) / 12.0
    slope = centred * (EPOCHS - 1) / total
    rate = jnp.sum(slope * pseudo, axis=0, keepdims=True)
    high = rate.astype(BF16).astype(F32)
    middle = (rate - high).astype(BF16).astype(F32)
    low = rate - high - middle
    row = iota((KPAD, IFGS), 0)
    full = jnp.where(row == EPOCHS, high, pseudo)
    full = jnp.where(row == EPOCHS + 1, middle, full)
    full = jnp.where(row == EPOCHS + 2, low, full)
    weights[...] = full.astype(BF16)


def kernel(
    phases, coherent_h, pairs_h, index_h, weight_h, cover_h, los_h, north_h,
    east_up, strain,
    sent, held, coherent, pairs, index, weight, cover, los, north,
    normal, weights, design, stack, rates, errors, offsets, shares, edge_out, edge_in,
    north_own, north_in, part_out, part_in, east_own, east_in,
    load_sem, small_sem, own_sem, send_sem, recv_sem, side_send, side_recv, part_send, part_recv,
):
    me = lax.axis_index("pix")
    track = lax.axis_index("track")
    after, before = lax.rem(me + 1, PIX), lax.rem(me + PIX - 1, PIX)
    right, left = lax.rem(track + 1, TRACKS), lax.rem(track + TRACKS - 1, TRACKS)

    def row_of(step):
        return lax.rem(GRD - step, GRD)

    def load(step):
        part = pl.ds(row_of(step) * TILES, TILES)
        return pltpu.make_async_copy(phases.at[:, part], sent.at[:, part], load_sem.at[step])

    small = [
        pltpu.make_async_copy(source, target, small_sem.at[i])
        for i, (source, target) in enumerate(
            (
                (coherent_h, coherent), (pairs_h, pairs), (index_h, index), (weight_h, weight),
                (cover_h, cover), (los_h, los), (north_h, north),
            )
        )
    ]
    small[0].start()
    for step in range(GRD):
        load(step).start()
    for copy in small[1:]:
        copy.start()

    barrier = pltpu.get_barrier_semaphore()

    def greet_pix(o, carry):
        pl.semaphore_signal(barrier, inc=1, device_id={"pix": lax.rem(me + o, PIX)}, device_id_type=MESH)
        return carry

    def greet_track(o, carry):
        pl.semaphore_signal(barrier, inc=1, device_id={"track": lax.rem(track + o, TRACKS)}, device_id_type=MESH)
        return carry

    lax.fori_loop(1, PIX, greet_pix, 0)
    lax.fori_loop(1, TRACKS, greet_track, 0)

    def mask(step):
        first = row_of(step) * TILES
        shift = lax.rem(LANES - first, LANES)

        def group(g, carry):
            flags = coherent[:, pl.ds(pl.multiple_of(g * LANES, LANES), LANES)]
            flags = pltpu.roll((flags == 1).astype(F32), shift, 1)
            for h in range(2):
                for t in range(TILES):
                    lane = h * (LANES // 2) + t
                    keep = jnp.broadcast_to(flags[:, lane : lane + 1], (LOCAL, LANES)).astype(BF16)
                    sent[2 * g + h, first + t] = sent[2 * g + h, first + t] * keep
            return carry

        lax.fori_loop(0, PIX // 2, group, 0)

    def ready(step):
        load(step).wait()
        mask(step)

    small[0].wait()
    ready(0)
    pl.semaphore_wait(barrier, PIX - 1 + TRACKS - 1)

    def send(step):
        part = pl.ds(row_of(step) * TILES, TILES)

        def to_peer(i, carry):
            o = PIX - 1 - i
            half = (o + 1) // 2
            peer = lax.rem(me + half + (o % 2) * (PIX - 2 * half), PIX)
            pltpu.make_async_remote_copy(
                src_ref=sent.at[peer, part],
                dst_ref=held.at[part, me],
                send_sem=send_sem,
                recv_sem=recv_sem.at[step],
                device_id={"pix": peer},
                device_id_type=MESH,
            ).start()
            return carry

        lax.fori_loop(0, PIX - 1, to_peer, 0)
        pltpu.make_async_copy(sent.at[me, part], held.at[part, me], own_sem.at[step]).start()

    send(0)

    def rest(step, carry):
        ready(step)
        send(step)
        return carry

    lax.fori_loop(1, GRD, rest, 0)
    for copy in small[1:]:
        copy.wait()

    north_own[...] = north[:, pl.ds(pl.multiple_of(track * LANES, LANES), LANES)]

    def side(source, target, slot, where):
        return pltpu.make_async_remote_copy(
            src_ref=source, dst_ref=target, send_sem=side_send.at[slot], recv_sem=side_recv.at[slot],
            device_id=where, device_id_type=MESH,
        )

    north_down = side(north_own, north_in.at[0], 0, {"pix": after})
    north_up = side(north_own, north_in.at[1], 1, {"pix": before})
    north_down.start()
    north_up.start()

    setup(pairs, normal, weights, design)

    for b in range(4):
        for i in range(GRD):
            offsets[b, i : i + 1, :] = index[b : b + 1, i * GCOLS : (i + 1) * GCOLS]
            shares[b, i : i + 1, :] = weight[b : b + 1, i * GCOLS : (i + 1) * GCOLS]

    def invert(step, carry):
        row = row_of(step)
        part = pl.ds(row * TILES, TILES)
        pltpu.make_async_copy(sent.at[me, part], held.at[part, me], own_sem.at[step]).wait()
        others = held.at[part, pl.ds(0, PIX - 1)]
        pltpu.make_async_copy(others, others, recv_sem.at[step]).wait()
        for t in range(TILES):
            stack[:, t * LANES : (t + 1) * LANES] = held[row * TILES + t].reshape(IFGS, LANES)
        series = jnp.dot(weights[...], stack[...], preferred_element_type=F32)
        rates[pl.ds(row, 1), :] = (
            series[EPOCHS : EPOCHS + 1] + series[EPOCHS + 1 : EPOCHS + 2] + series[EPOCHS + 2 : EPOCHS + 3]
        )
        fitted = jnp.dot(design[...], series.astype(BF16), preferred_element_type=F32)
        misfit = stack[...].astype(F32) - fitted
        errors[pl.ds(row, 1), :] = jnp.sum(misfit * misfit, axis=0, keepdims=True) / IFGS
        return carry

    lax.fori_loop(0, 2, invert, 0)
    edge_out[0, 0] = rates[:, GCOLS - LANES :]
    edge_out[0, 1] = errors[:, GCOLS - LANES :]
    edge_out[1, 0] = rates[:, :LANES]
    edge_out[1, 1] = errors[:, :LANES]
    edge_down = side(edge_out.at[0], edge_in.at[0], 2, {"pix": after})
    edge_up = side(edge_out.at[1], edge_in.at[1], 3, {"pix": before})
    edge_down.start()
    edge_up.start()
    lax.fori_loop(2, GRD, invert, 0)
    edge_down.wait()
    edge_up.wait()

    lane = iota((GRD, LANES), 1)
    row = iota((GRD, LANES), 0)
    lane_los = iota((1, TRACKS), 1)
    north_c = jnp.sum(jnp.where(lane_los == track, los[1:2, :], 0.0), axis=1, keepdims=True)
    covered = cover[...].astype(F32)
    for k in range(TILES):
        span = slice(k * LANES, (k + 1) * LANES)
        picked = [jnp.zeros((GRD, LANES), F32)] * 2
        total = jnp.zeros((GRD, LANES), F32)
        tiles = []
        for f, field in enumerate((rates, errors)):
            if k > 0:
                prev = field[:, (k - 1) * LANES : k * LANES]
            else:
                prev = pltpu.roll(field[:, GCOLS - LANES :], 1, 0)
                prev = jnp.where(row == 0, pltpu.roll(edge_in[0, f], 1, 0), prev)
            if k < TILES - 1:
                later = field[:, (k + 1) * LANES : (k + 2) * LANES]
            else:
                later = pltpu.roll(field[:, :LANES], GRD - 1, 0)
                later = jnp.where(row == GRD - 1, pltpu.roll(edge_in[1, f], GRD - 1, 0), later)
            tiles.append((prev, field[:, span], later))
        for b in range(4):
            place = lane + offsets[b, :, span]
            inner = place & (LANES - 1)
            share = shares[b, :, span]
            total = total + share
            for f in range(2):
                options = [jnp.take_along_axis(tile, inner, axis=1) for tile in tiles[f]]
                value = jnp.where(place < 0, options[0], jnp.where(place >= LANES, options[2], options[1]))
                picked[f] = picked[f] + value * share
        part_out[k, 0] = covered[:, k : k + 1] / (picked[1] / total + prior_var)
        part_out[k, 1] = picked[0] / total - north_c * north[:, span]

    def part(o):
        peer = lax.rem(track + o, TRACKS)
        return pltpu.make_async_remote_copy(
            src_ref=part_out.at[peer], dst_ref=part_in.at[track], send_sem=part_send, recv_sem=part_recv,
            device_id={"track": peer}, device_id_type=MESH,
        )

    for o in range(1, TRACKS):
        part(o).start()
    part_in[track] = part_out[track]
    seven = part_in.at[pl.ds(0, TRACKS - 1)]
    pltpu.make_async_copy(seven, seven, part_recv).wait()

    a11 = jnp.full((GRD, LANES), ridge_term, F32)
    a22 = jnp.full((GRD, LANES), ridge_term, F32)
    a12 = jnp.zeros((GRD, LANES), F32)
    b1 = jnp.zeros((GRD, LANES), F32)
    b2 = jnp.zeros((GRD, LANES), F32)
    for t in range(TRACKS):
        w, y = part_in[t, 0], part_in[t, 1]
        e, u = los[0:1, t : t + 1], los[2:3, t : t + 1]
        we, wu = w * e, w * u
        a11, a12, a22 = a11 + we * e, a12 + we * u, a22 + wu * u
        b1, b2 = b1 + we * y, b2 + wu * y
    determ = a11 * a22 - a12 * a12
    east = (a22 * b1 - a12 * b2) / determ
    east_own[...] = east
    sides = [
        side(east_own, east_in.at[0], 4, {"pix": after}),
        side(east_own, east_in.at[1], 5, {"pix": before}),
        side(east_own, east_in.at[2], 6, {"track": right}),
        side(east_own, east_in.at[3], 7, {"track": left}),
    ]
    for copy in sides:
        copy.start()
    east_up[0] = east
    east_up[1] = (a11 * b2 - a12 * b1) / determ

    pix_first, pix_last = me == 0, me == PIX - 1
    north_down.wait()
    north_up.wait()
    mine = north_own[...]
    above, below = pltpu.roll(north_in[0], 1, 0), pltpu.roll(north_in[1], GRD - 1, 0)
    above = jnp.where(pix_first, 0.0, above)
    below = jnp.where(pix_last, 0.0, below)
    north_m = jnp.where(row == 0, above, pltpu.roll(mine, 1, 0))
    north_p = jnp.where(row == GRD - 1, below, pltpu.roll(mine, GRD - 1, 0))
    west = north[:, pl.ds(pl.multiple_of(left * LANES, LANES), LANES)]
    orient = north[:, pl.ds(pl.multiple_of(right * LANES, LANES), LANES)]
    west = jnp.where(track == 0, 0.0, pltpu.roll(west, 1, 1))
    orient = jnp.where(track == TRACKS - 1, 0.0, pltpu.roll(orient, LANES - 1, 1))
    north_l = jnp.where(lane == 0, west, pltpu.roll(mine, 1, 1))
    north_r = jnp.where(lane == LANES - 1, orient, pltpu.roll(mine, LANES - 1, 1))
    strain[1] = (north_p - north_m) / 2.0

    for copy in sides:
        copy.wait()
    above, below = pltpu.roll(east_in[0], 1, 0), pltpu.roll(east_in[1], GRD - 1, 0)
    above = jnp.where(pix_first, 0.0, above)
    below = jnp.where(pix_last, 0.0, below)
    west = jnp.where(track == 0, 0.0, pltpu.roll(east_in[2], 1, 1))
    orient = jnp.where(track == TRACKS - 1, 0.0, pltpu.roll(east_in[3], LANES - 1, 1))
    east_m = jnp.where(row == 0, above, pltpu.roll(east, 1, 0))
    east_p = jnp.where(row == GRD - 1, below, pltpu.roll(east, GRD - 1, 0))
    east_l = jnp.where(lane == 0, west, pltpu.roll(east, 1, 1))
    east_r = jnp.where(lane == LANES - 1, orient, pltpu.roll(east, LANES - 1, 1))
    strain[0] = (east_r - east_l) / 2.0
    strain[2] = (east_p - east_m + north_r - north_l) / 4.0

    pltpu.make_async_copy(seven, seven, part_send).wait()
    others = sent.at[pl.ds(0, PIX - 1)]
    pltpu.make_async_copy(others, others, send_sem).wait()


def per_device(phases, coherent, pairs, res_index, res_weight, coverage, los, north):
    tiles = phases.shape[2] // PIX // LANES
    stack = phases[0].reshape(LOCAL, PIX, tiles, LANES).transpose(1, 2, 0, 3)
    hbm = pl.BlockSpec(memory_space=pl.ANY)
    vmem = pl.BlockSpec(memory_space=pltpu.VMEM)
    dma = pltpu.SemaphoreType.DMA
    width = GRD * GCOLS
    return pl.pallas_call(
        kernel,
        out_shape=(
            jax.ShapeDtypeStruct((2, GRD, LANES), F32),
            jax.ShapeDtypeStruct((3, GRD, LANES), F32),
        ),
        in_specs=[hbm] * 8,
        out_specs=(vmem, vmem),
        scratch_shapes=[
            pltpu.VMEM((PIX, tiles, LOCAL, LANES), BF16),
            pltpu.VMEM((tiles, PIX, LOCAL, LANES), BF16),
            pltpu.VMEM(coherent.shape[1:], jnp.int32),
            pltpu.VMEM((2, IFGS), jnp.int32),
            pltpu.VMEM((4, width), jnp.int32),
            pltpu.VMEM((4, width), F32),
            pltpu.VMEM((GRD, TILES), jnp.int32),
            pltpu.VMEM((3, TRACKS), F32),
            pltpu.VMEM((GRD, GCOLS), F32),
            pltpu.VMEM((KPAD, KPAD), F32),
            pltpu.VMEM((KPAD, IFGS), BF16),
            pltpu.VMEM((IFGS, KPAD), BF16),
            pltpu.VMEM((IFGS, GCOLS), BF16),
            pltpu.VMEM((GRD, GCOLS), F32),
            pltpu.VMEM((GRD, GCOLS), F32),
            pltpu.VMEM((4, GRD, GCOLS), jnp.int32),
            pltpu.VMEM((4, GRD, GCOLS), F32),
            pltpu.VMEM((2, 2, GRD, LANES), F32),
            pltpu.VMEM((2, 2, GRD, LANES), F32),
            pltpu.VMEM((GRD, LANES), F32),
            pltpu.VMEM((2, GRD, LANES), F32),
            pltpu.VMEM((TRACKS, 2, GRD, LANES), F32),
            pltpu.VMEM((TRACKS, 2, GRD, LANES), F32),
            pltpu.VMEM((GRD, LANES), F32),
            pltpu.VMEM((4, GRD, LANES), F32),
            dma((GRD,)),
            dma((7,)),
            dma((GRD,)),
            dma(()),
            dma((GRD,)),
            dma((8,)),
            dma((8,)),
            dma(()),
            dma(()),
        ],
        compiler_params=pltpu.CompilerParams(collective_id=0, has_side_effects=True),
    )(stack, coherent[0], pairs[0].T, res_index[0], res_weight[0], coverage[0], los.T, north)


def solution(mesh):
    in_specs = (
        P("track", "pix", None),
        P("track", "pix", None),
        P("track", None, None),
        P("track", None, "pix"),
        P("track", None, "pix"),
        P("track", "pix", None),
        P(),
        P("pix", None),
    )
    out_specs = (P(None, "pix", "track"), P(None, "pix", "track"))
    return jax.shard_map(
        per_device, mesh=mesh, in_specs=in_specs, out_specs=out_specs, check_vma=False
    )
```

time: 437 us -> 216 us (0.49)
  Pallas kernels: 0 us -> 210 us
  local copies, waits for them, and re-layouts: 153 us -> 2.6 us
  waiting for transfers between devices: 146 us -> 0 us
  other arithmetic: 76.5 us -> 0 us
  starting transfers between devices: 43.7 us -> 0 us
  matrix products: 11.1 us -> 0 us
    pallas_call x0 -> x1, Pallas kernels: none -> 210 us  [per_device(): pl.pallas_call(kernel, out_shape=(jax.ShapeDtypeStruct((2, GRD, LANES), F...]
    all_to_all x3 -> x0, waiting for transfers between devices: 137 us -> none  [the longest x1 134 us: per_device(): lax.all_to_all(masked, 'pix', split_axis=1, concat_axis=0, tiled=True)]
    gather x1 -> x0, local copies, waits for them, and re-layouts: 110 us -> none  [per_device(): picked = jnp.take(extended, local, axis=1)]
    another operation x17 -> x0, other arithmetic: 50.5 us -> none  [the longest x7 29.4 us: setup_track(): factor = jnp.linalg.cholesky(normal)]
    all_to_all x3 -> x0, starting transfers between devices: 28.9 us -> none  [the longest x1 19.1 us: per_device(): lax.all_to_all(masked, 'pix', split_axis=1, concat_axis=0, tiled=True)]
    reduce_sum x4 -> x0, other arithmetic: 15.6 us -> none  [the longest x2 14.8 us: per_device(): grid = jnp.sum(picked * weight[None], axis=1) / jnp.sum(weight, axis=0)]
    ppermute x6 -> x0, starting transfers between devices: 14.9 us -> none  [the longest x3 8.66 us: with_halo(): before = lax.ppermute(last, axis, up)]
    broadcast_in_dim x3 -> x0, local copies, waits for them, and re-layouts: 13 us -> none  [the longest x2 13 us: per_device(): jnp.where(coherent[0][:, :, None] == 1, blocked, jnp.zeros((), jnp.bfloat...]
  transfers between devices with their start and end apart: 9 -> 0, of which waited for: 5 -> 0; matrix products, arithmetic and copies ran while one was open for 48% -> 0% of each run, Pallas kernels for 0% -> 0%
where the time goes in v1:
time: 216 us; the launch traced here: 213 us
  Pallas kernels  210 us (97%)
  local copies, waits for them, and re-layouts  2.6 us (1%)
    pallas_call x1, Pallas kernels, per_device(): pl.pallas_call(kernel, out_shape=(jax.ShapeDtypeStruct((2, GRD, LANES), F...  210 us

profile of v1, /device:TPU:24, one launch (start us, length us, event | category | flops | bytes accessed | tf_op | source)
XLA Modules:
  0.0 213.3 jit_solution(1431449968525004964)
XLA Ops:
  0.6 210.1 %shard_map.95 = (f32[2,8,128]{2,1,0:T(8,128)}, f32[3,8,128]{2,1,0:T(8,128)}) custom-call(bf16[64,64,4,128]{3,2,1,0:T(4,128)(2,1)} %bitcast.11, s32[4,4096]{1,0:T(4,128)} %bitcast.14, s32[2,256]{1,0:T(2,128)} %bitcast.16, s32[4,8192]{1,0:T(4,128)} %bitcast.12, f32[4,8192]{1,0:T(4,128)} %bitcast.13, s32[8,8]{1,0:T(8,128)} %bitcast.15, f32[3,8]{1,0:T(4,128)} %bitcast.17, ...), custom_call_target="tpu_custom_call" | custom-call | tf_op jit(solution)/shard_map/pallas_call | solution.py:338
  210.7 1.3 copy.12
  212.0 1.3 copy.13

commit v2 on v1

v2 whole, which is shorter than its diff:
```python
import jax
import jax.numpy as jnp
from jax import lax
from jax.experimental import pallas as pl
from jax.experimental.pallas import tpu as pltpu
from jax.sharding import PartitionSpec as P

IFGS = 256
EPOCHS = 200
GRD = 8
GCOLS = 1024
LANES = 128
TILES = GCOLS // LANES
PIX = 64
TRACKS = 8
RING = 4
RINGS = PIX // RING
REACH = 4
EARLY = 2
LOCAL = IFGS // PIX
KPAD = 256
BATCH = 4

prior_var = 0.1
ridge_term = 0.5

MESH = pl.DeviceIdType.MESH
F32 = jnp.float32
BF16 = jnp.bfloat16
HIGHEST = lax.Precision.HIGHEST


def iota(shape, dim):
    return lax.broadcasted_iota(jnp.int32, shape, dim)


def setup(pairs, normal, weights, design):
    epoch = iota((KPAD, IFGS), 0)
    design_t = (epoch == pairs[1:2, :]).astype(F32) - (epoch == pairs[0:1, :]).astype(F32)
    design[...] = design_t.T.astype(BF16)
    gram = lax.dot_general(
        design_t.astype(BF16), design_t.astype(BF16), (((1,), (1,)), ((), ())), preferred_element_type=F32
    )
    normal[...] = gram + (iota((KPAD, KPAD), 0) == iota((KPAD, KPAD), 1)).astype(F32)

    def eliminate(k, carry):
        row = normal[pl.ds(k, 1), :]
        here = iota((1, KPAD), 1) == k
        inverse = 1.0 / jnp.sum(jnp.where(here, row, 0.0), axis=1, keepdims=True)
        scaled = jnp.where(here, inverse, row * inverse)
        block = normal[0:EPOCHS, :]
        at_k = iota((EPOCHS, KPAD), 1) == k
        column = jnp.sum(jnp.where(at_k, block, 0.0), axis=1, keepdims=True)
        normal[0:EPOCHS, :] = jnp.where(at_k, 0.0, block) - column * scaled
        normal[pl.ds(k, 1), :] = scaled
        return carry

    lax.fori_loop(0, EPOCHS, eliminate, 0)
    pseudo = jnp.dot(normal[...], design_t, precision=HIGHEST, preferred_element_type=F32)
    pseudo = jnp.where(iota((KPAD, IFGS), 0) < EPOCHS, pseudo, 0.0).astype(BF16).astype(F32)
    centred = iota((KPAD, 1), 0).astype(F32) - (EPOCHS - 1) / 2.0
    total = EPOCHS * (EPOCHS * EPOCHS - 1) / 12.0
    slope = centred * (EPOCHS - 1) / total
    rate = jnp.sum(slope * pseudo, axis=0, keepdims=True)
    high = rate.astype(BF16).astype(F32)
    middle = (rate - high).astype(BF16).astype(F32)
    low = rate - high - middle
    row = iota((KPAD, IFGS), 0)
    full = jnp.where(row == EPOCHS, high, pseudo)
    full = jnp.where(row == EPOCHS + 1, middle, full)
    full = jnp.where(row == EPOCHS + 2, low, full)
    weights[...] = full.astype(BF16)


def kernel(
    phases, coherent_h, pairs_h, index_h, weight_h, cover_h, los_h, north_h,
    result,
    sent, held, coherent, pairs, index, weight, cover, los, north,
    normal, weights, design, stack, rates, errors, offsets, shares, covered, edge_out, edge_in,
    north_own, north_in, part_out, part_in, east_own, east_in,
    load_sem, small_sem, own_sem, send_sem, recv_sem, side_send, side_recv, part_send, part_recv, relay_sem,
):
    me = lax.axis_index("pix")
    track = lax.axis_index("track")
    after, before = lax.rem(me + 1, PIX), lax.rem(me + PIX - 1, PIX)
    right, left = lax.rem(track + 1, TRACKS), lax.rem(track + TRACKS - 1, TRACKS)

    def tile_of(step):
        return lax.rem(step + TILES - 1, TILES)

    def load(step):
        k = tile_of(step)
        return pltpu.make_async_copy(phases.at[:, :, k], sent.at[k], load_sem.at[step])

    small = [
        pltpu.make_async_copy(source, target, small_sem.at[i])
        for i, (source, target) in enumerate(
            (
                (coherent_h, coherent), (pairs_h, pairs), (index_h, index), (weight_h, weight),
                (cover_h, cover), (los_h, los), (north_h, north),
            )
        )
    ]
    small[0].start()
    for step in range(TILES):
        load(step).start()
    for copy in small[1:]:
        copy.start()

    barrier = pltpu.get_barrier_semaphore()

    def at(down, over):
        return lax.rem(me // RING + down, RINGS) * RING + lax.rem(me % RING + over, RING)

    def near(i):
        n = 2 * REACH - 1 - i // RING
        half = n // 2 + 1
        return at(half + (1 - n % 2) * (RINGS - 2 * half), i % RING)

    def far(i):
        n = RINGS - 2 * REACH - 2 - i // RING
        half = REACH + 1 + n // 2
        return at(half + (1 - n % 2) * (RINGS - 2 * half), i % RING)

    def greet(peer):
        pl.semaphore_signal(barrier, inc=1, device_id={"pix": peer}, device_id_type=MESH)

    def greet_near(i, carry):
        greet(near(i))
        return carry

    def greet_track(o, carry):
        pl.semaphore_signal(barrier, inc=1, device_id={"track": lax.rem(track + o, TRACKS)}, device_id_type=MESH)
        return carry

    lax.fori_loop(0, 2 * REACH * RING, greet_near, 0)
    for over in range(1, RING):
        greet(at(0, over))
    lax.fori_loop(1, TRACKS, greet_track, 0)

    def mask(k, shift, groups):
        kept = []
        for g in groups:
            flags = coherent[:, pl.ds(pl.multiple_of(g * LANES, LANES), LANES)]
            flags = pltpu.roll((flags == 1).astype(F32), shift, 1)
            for h in range(2):
                for i in range(GRD):
                    lane = h * (LANES // 2) + i * TILES
                    keep = jnp.broadcast_to(flags[:, lane : lane + 1], (LOCAL, LANES)).astype(BF16)
                    kept.append((2 * g + h, i, sent[k, 2 * g + h, i] * keep))
        for peer, i, value in kept:
            sent[k, peer, i] = value

    def send(step, k, peer):
        pltpu.make_async_remote_copy(
            src_ref=sent.at[k, peer],
            dst_ref=held.at[k, :, me],
            send_sem=send_sem,
            recv_sem=recv_sem.at[step],
            device_id={"pix": peer},
            device_id_type=MESH,
        ).start()

    def own(step, k):
        return pltpu.make_async_copy(sent.at[k, me], held.at[k, :, me], own_sem.at[step])

    def ready(step):
        load(step).wait()
        k = tile_of(step)
        shift = lax.rem(LANES - k, LANES)

        def group(g, carry):
            mask(k, shift, [BATCH * g + m for m in range(BATCH)])
            return carry

        lax.fori_loop(0, PIX // 2 // BATCH, group, 0)

    def send_near(step):
        k = tile_of(step)

        def to_peer(i, carry):
            send(step, k, near(i))
            return carry

        lax.fori_loop(0, 2 * REACH * RING, to_peer, 0)
        for over in range(1, RING):
            send(step, k, at(0, over))

    def send_far(step):
        k = tile_of(step)

        def to_peer(i, carry):
            send(step, k, far(i))
            return carry

        lax.fori_loop(0, (RINGS - 2 * REACH - 1) * RING, to_peer, 0)
        own(step, k).start()

    def rest(step, carry):
        ready(step)
        send_far(step)
        send_near(step)
        return carry

    small[0].wait()
    ready(0)
    pl.semaphore_wait(barrier, (2 * REACH + 1) * RING - 1 + TRACKS - 1)
    for down in (REACH, RINGS - REACH):
        pl.semaphore_signal(relay_sem, inc=1, device_id={"pix": at(down, 0)}, device_id_type=MESH)
    for step in range(EARLY):
        if step:
            ready(step)
        send_near(step)
    pl.semaphore_wait(relay_sem, 2)
    for step in range(EARLY):
        send_far(step)
    lax.fori_loop(EARLY, TILES, rest, 0)
    for copy in small[1:]:
        copy.wait()

    north_own[...] = north[:, pl.ds(pl.multiple_of(track * LANES, LANES), LANES)]

    def side(source, target, slot, where):
        return pltpu.make_async_remote_copy(
            src_ref=source, dst_ref=target, send_sem=side_send.at[slot], recv_sem=side_recv.at[slot],
            device_id=where, device_id_type=MESH,
        )

    north_down = side(north_own, north_in.at[0], 0, {"pix": after})
    north_up = side(north_own, north_in.at[1], 1, {"pix": before})
    north_down.start()
    north_up.start()

    setup(pairs, normal, weights, design)

    lane = iota((GRD, LANES), 1)
    row = iota((GRD, LANES), 0)
    flags = cover[...].astype(F32)
    for k in range(TILES):
        covered[k] = jnp.broadcast_to(flags[:, k : k + 1], (GRD, LANES))
        for b in range(4):
            for i in range(GRD):
                begin = i * GCOLS + k * LANES
                offsets[k, b, i : i + 1, :] = index[b : b + 1, begin : begin + LANES] + lane[:1]
                shares[k, b, i : i + 1, :] = weight[b : b + 1, begin : begin + LANES]
    lane_los = iota((1, TRACKS), 1)
    north_c = jnp.sum(jnp.where(lane_los == track, los[1:2, :], 0.0), axis=1, keepdims=True)

    def invert(step):
        k = tile_of(step)
        own(step, k).wait()
        others = held.at[k, :, pl.ds(0, PIX - 1)]
        pltpu.make_async_copy(others, others, recv_sem.at[step]).wait()
        for i in range(GRD):
            stack[:, i * LANES : (i + 1) * LANES] = held[k, i].reshape(IFGS, LANES)
        series = jnp.dot(weights[...], stack[...], preferred_element_type=F32)
        rate = series[EPOCHS : EPOCHS + 1] + series[EPOCHS + 1 : EPOCHS + 2] + series[EPOCHS + 2 : EPOCHS + 3]
        fitted = jnp.dot(design[...], series.astype(BF16), preferred_element_type=F32)
        misfit = stack[...].astype(F32) - fitted
        error = jnp.sum(misfit * misfit, axis=0, keepdims=True) / IFGS
        for i in range(GRD):
            rates[k + 1, i : i + 1, :] = rate[:, i * LANES : (i + 1) * LANES]
            errors[k + 1, i : i + 1, :] = error[:, i * LANES : (i + 1) * LANES]

    def part(k):
        return pltpu.make_async_remote_copy(
            src_ref=part_out.at[k], dst_ref=part_in.at[track], send_sem=part_send, recv_sem=part_recv,
            device_id={"track": k}, device_id_type=MESH,
        )

    def resample(k):
        tiles = [[field[k + n] for n in range(3)] for field in (rates, errors)]
        picked = [jnp.zeros((GRD, LANES), F32)] * 2
        total = jnp.zeros((GRD, LANES), F32)
        for b in range(4):
            place = offsets[k, b]
            inner = place & (LANES - 1)
            share = shares[k, b]
            total = total + share
            for f in range(2):
                options = [jnp.take_along_axis(tile, inner, axis=1) for tile in tiles[f]]
                value = jnp.where(place < 0, options[0], jnp.where(place >= LANES, options[2], options[1]))
                picked[f] = picked[f] + value * share
        part_out[k, 0] = covered[k] / (picked[1] / total + prior_var)
        part_out[k, 1] = picked[0] / total - north_c * north[:, pl.ds(pl.multiple_of(k * LANES, LANES), LANES)]

        @pl.when(k != track)
        def _():
            part(k).start()

    invert(0)
    invert(1)
    edge_out[0, 0] = rates[TILES]
    edge_out[0, 1] = errors[TILES]
    edge_out[1, 0] = rates[1]
    edge_out[1, 1] = errors[1]
    edge_down = side(edge_out.at[0], edge_in.at[0], 2, {"pix": after})
    edge_up = side(edge_out.at[1], edge_in.at[1], 3, {"pix": before})
    edge_down.start()
    edge_up.start()
    invert(2)
    edge_down.wait()
    edge_up.wait()
    for f, field in enumerate((rates, errors)):
        field[0] = jnp.where(row == 0, pltpu.roll(edge_in[0, f], 1, 0), pltpu.roll(field[TILES], 1, 0))
        field[TILES + 1] = jnp.where(
            row == GRD - 1, pltpu.roll(edge_in[1, f], GRD - 1, 0), pltpu.roll(field[1], GRD - 1, 0)
        )
    resample(0)

    def advance(step, carry):
        invert(step)
        resample(step - 2)
        return carry

    lax.fori_loop(3, TILES, advance, 0)
    resample(TILES - 2)
    resample(TILES - 1)
    part_in[track] = part_out[track]
    seven = part_in.at[pl.ds(0, TRACKS - 1)]
    pltpu.make_async_copy(seven, seven, part_recv).wait()

    a11 = jnp.full((GRD, LANES), ridge_term, F32)
    a22 = jnp.full((GRD, LANES), ridge_term, F32)
    a12 = jnp.zeros((GRD, LANES), F32)
    b1 = jnp.zeros((GRD, LANES), F32)
    b2 = jnp.zeros((GRD, LANES), F32)
    for t in range(TRACKS):
        w, y = part_in[t, 0], part_in[t, 1]
        e, u = los[0:1, t : t + 1], los[2:3, t : t + 1]
        we, wu = w * e, w * u
        a11, a12, a22 = a11 + we * e, a12 + we * u, a22 + wu * u
        b1, b2 = b1 + we * y, b2 + wu * y
    determ = a11 * a22 - a12 * a12
    east = (a22 * b1 - a12 * b2) / determ
    east_own[...] = east
    sides = [
        side(east_own, east_in.at[0], 4, {"pix": after}),
        side(east_own, east_in.at[1], 5, {"pix": before}),
        side(east_own, east_in.at[2], 6, {"track": right}),
        side(east_own, east_in.at[3], 7, {"track": left}),
    ]
    for copy in sides:
        copy.start()
    result[0] = east
    result[1] = (a11 * b2 - a12 * b1) / determ

    pix_first, pix_last = me == 0, me == PIX - 1
    north_down.wait()
    north_up.wait()
    mine = north_own[...]
    above, below = pltpu.roll(north_in[0], 1, 0), pltpu.roll(north_in[1], GRD - 1, 0)
    above = jnp.where(pix_first, 0.0, above)
    below = jnp.where(pix_last, 0.0, below)
    north_m = jnp.where(row == 0, above, pltpu.roll(mine, 1, 0))
    north_p = jnp.where(row == GRD - 1, below, pltpu.roll(mine, GRD - 1, 0))
    west = north[:, pl.ds(pl.multiple_of(left * LANES, LANES), LANES)]
    orient = north[:, pl.ds(pl.multiple_of(right * LANES, LANES), LANES)]
    west = jnp.where(track == 0, 0.0, pltpu.roll(west, 1, 1))
    orient = jnp.where(track == TRACKS - 1, 0.0, pltpu.roll(orient, LANES - 1, 1))
    north_l = jnp.where(lane == 0, west, pltpu.roll(mine, 1, 1))
    north_r = jnp.where(lane == LANES - 1, orient, pltpu.roll(mine, LANES - 1, 1))
    result[3] = (north_p - north_m) / 2.0

    for copy in sides:
        copy.wait()
    above, below = pltpu.roll(east_in[0], 1, 0), pltpu.roll(east_in[1], GRD - 1, 0)
    above = jnp.where(pix_first, 0.0, above)
    below = jnp.where(pix_last, 0.0, below)
    west = jnp.where(track == 0, 0.0, pltpu.roll(east_in[2], 1, 1))
    orient = jnp.where(track == TRACKS - 1, 0.0, pltpu.roll(east_in[3], LANES - 1, 1))
    east_m = jnp.where(row == 0, above, pltpu.roll(east, 1, 0))
    east_p = jnp.where(row == GRD - 1, below, pltpu.roll(east, GRD - 1, 0))
    east_l = jnp.where(lane == 0, west, pltpu.roll(east, 1, 1))
    east_r = jnp.where(lane == LANES - 1, orient, pltpu.roll(east, LANES - 1, 1))
    result[2] = (east_r - east_l) / 2.0
    result[4] = (east_p - east_m + north_r - north_l) / 4.0

    pltpu.make_async_copy(seven, seven, part_send).wait()
    others = sent.at[:, pl.ds(0, PIX - 1)]
    pltpu.make_async_copy(others, others, send_sem).wait()


def deliver(result, east_up, strain):
    east_up[...] = result[0:2]
    strain[...] = result[2:5]


def per_device(phases, coherent, pairs, res_index, res_weight, coverage, los, north):
    stack = phases[0].reshape(LOCAL, PIX, GRD, TILES, LANES).transpose(1, 2, 3, 0, 4)
    hbm = pl.BlockSpec(memory_space=pl.ANY)
    vmem = pl.BlockSpec(memory_space=pltpu.VMEM)
    dma = pltpu.SemaphoreType.DMA
    width = GRD * GCOLS
    tile = (GRD, LANES)
    result = pl.pallas_call(
        kernel,
        out_shape=jax.ShapeDtypeStruct((5, *tile), F32),
        in_specs=[hbm] * 8,
        out_specs=vmem,
        scratch_shapes=[
            pltpu.VMEM((TILES, PIX, GRD, LOCAL, LANES), BF16),
            pltpu.VMEM((TILES, GRD, PIX, LOCAL, LANES), BF16),
            pltpu.VMEM(coherent.shape[1:], jnp.int32),
            pltpu.VMEM((2, IFGS), jnp.int32),
            pltpu.VMEM((4, width), jnp.int32),
            pltpu.VMEM((4, width), F32),
            pltpu.VMEM((GRD, TILES), jnp.int32),
            pltpu.VMEM((3, TRACKS), F32),
            pltpu.VMEM((GRD, GCOLS), F32),
            pltpu.VMEM((KPAD, KPAD), F32),
            pltpu.VMEM((KPAD, IFGS), BF16),
            pltpu.VMEM((IFGS, KPAD), BF16),
            pltpu.VMEM((IFGS, GCOLS), BF16),
            pltpu.VMEM((TILES + 2, *tile), F32),
            pltpu.VMEM((TILES + 2, *tile), F32),
            pltpu.VMEM((TILES, 4, *tile), jnp.int32),
            pltpu.VMEM((TILES, 4, *tile), F32),
            pltpu.VMEM((TILES, *tile), F32),
            pltpu.VMEM((2, 2, *tile), F32),
            pltpu.VMEM((2, 2, *tile), F32),
            pltpu.VMEM(tile, F32),
            pltpu.VMEM((2, *tile), F32),
            pltpu.VMEM((TRACKS, 2, *tile), F32),
            pltpu.VMEM((TRACKS, 2, *tile), F32),
            pltpu.VMEM(tile, F32),
            pltpu.VMEM((4, *tile), F32),
            dma((TILES,)),
            dma((7,)),
            dma((TILES,)),
            dma(()),
            dma((TILES,)),
            dma((8,)),
            dma((8,)),
            dma(()),
            dma(()),
            pltpu.SemaphoreType.REGULAR,
        ],
        compiler_params=pltpu.CompilerParams(collective_id=0, has_side_effects=True),
    )(stack, coherent[0], pairs[0].T, res_index[0], res_weight[0], coverage[0], los.T, north)
    return pl.pallas_call(
        deliver,
        out_shape=(jax.ShapeDtypeStruct((2, *tile), F32), jax.ShapeDtypeStruct((3, *tile), F32)),
        in_specs=[vmem],
        out_specs=(vmem, vmem),
    )(result)


def solution(mesh):
    in_specs = (
        P("track", "pix", None),
        P("track", "pix", None),
        P("track", None, None),
        P("track", None, "pix"),
        P("track", None, "pix"),
        P("track", "pix", None),
        P(),
        P("pix", None),
    )
    out_specs = (P(None, "pix", "track"), P(None, "pix", "track"))
    return jax.shard_map(
        per_device, mesh=mesh, in_specs=in_specs, out_specs=out_specs, check_vma=False
    )
```

time: 216 us -> 212 us (0.981); the launches traced: 213 us -> 212 us
  local copies, waits for them, and re-layouts: 2.6 us -> 0 us
    unnamed x2 -> x0, local copies, waits for them, and re-layouts: 2.6 us -> none
    pallas_call x1 -> x2, Pallas kernels: 210 us -> 211 us  [the longest x1 210 us: per_device(): pl.pallas_call(kernel, out_shape=jax.ShapeDtypeStruct((5, *tile), F32), i...]
where the time goes in v2:
time: 212 us
  Pallas kernels  211 us (100%)
    pallas_call x1, Pallas kernels, per_device(): pl.pallas_call(kernel, out_shape=jax.ShapeDtypeStruct((5, *tile), F32), i...  210 us

profile of v2, /device:TPU:24, one launch (start us, length us, event | category | flops | bytes accessed | tf_op | source)
XLA Modules:
  0.0 211.8 jit_solution(13696321381722689225)
XLA Ops:
  0.6 209.8 %shard_map.95.result = f32[5,8,128]{2,1,0:T(8,128)} custom-call(bf16[64,8,8,4,128]{4,3,2,1,0:T(4,128)(2,1)} %bitcast.11, s32[4,4096]{1,0:T(4,128)} %bitcast.14, s32[2,256]{1,0:T(2,128)} %bitcast.16, s32[4,8192]{1,0:T(4,128)} %bitcast.12, f32[4,8192]{1,0:T(4,128)} %bitcast.13, s32[8,8]{1,0:T(8,128)} %bitcast.15, f32[3,8]{1,0:T(4,128)} %bitcast.17, ...), custom_call_target="tpu_custom_call" | custom-call | tf_op jit(solution)/shard_map/pallas_call | solution.py:396
  210.5 1.3 shard_map.96

commit v3 on v2

--- a/solution.py
+++ b/solution.py
@@ -268,7 +268,7 @@
             device_id={"track": k}, device_id_type=MESH,
         )
 
-    def resample(k):
+    def resampled(k):
         tiles = [[field[k + n] for n in range(3)] for field in (rates, errors)]
         picked = [jnp.zeros((GRD, LANES), F32)] * 2
         total = jnp.zeros((GRD, LANES), F32)
@@ -281,12 +281,19 @@
                 options = [jnp.take_along_axis(tile, inner, axis=1) for tile in tiles[f]]
                 value = jnp.where(place < 0, options[0], jnp.where(place >= LANES, options[2], options[1]))
                 picked[f] = picked[f] + value * share
-        part_out[k, 0] = covered[k] / (picked[1] / total + prior_var)
-        part_out[k, 1] = picked[0] / total - north_c * north[:, pl.ds(pl.multiple_of(k * LANES, LANES), LANES)]
-
-        @pl.when(k != track)
-        def _():
-            part(k).start()
+        own_north = north[:, pl.ds(pl.multiple_of(k * LANES, LANES), LANES)]
+        return covered[k] / (picked[1] / total + prior_var), picked[0] / total - north_c * own_north
+
+    def resample(*several):
+        values = [resampled(k) for k in several]
+        for k, (weight_k, y_k) in zip(several, values):
+            part_out[k, 0] = weight_k
+            part_out[k, 1] = y_k
+        for k in several:
+
+            @pl.when(k != track)
+            def _(k=k):
+                part(k).start()
 
     invert(0)
     invert(1)
@@ -313,9 +320,9 @@
         resample(step - 2)
         return carry
 
-    lax.fori_loop(3, TILES, advance, 0)
-    resample(TILES - 2)
-    resample(TILES - 1)
+    lax.fori_loop(3, TILES - 1, advance, 0)
+    invert(TILES - 1)
+    resample(TILES - 3, TILES - 2, TILES - 1)
     part_in[track] = part_out[track]
     seven = part_in.at[pl.ds(0, TRACKS - 1)]
     pltpu.make_async_copy(seven, seven, part_recv).wait()

time: 212 us -> 212 us (level)
  no operation moved by 1% of the time
where the time goes in v3:
time: 212 us
  Pallas kernels  211 us (100%)
    pallas_call x1, Pallas kernels, per_device(): pl.pallas_call(kernel, out_shape=jax.ShapeDtypeStruct((5, *tile), F32), i...  210 us

profile of v3, /device:TPU:24, one launch (start us, length us, event | category | flops | bytes accessed | tf_op | source)
XLA Modules:
  0.0 211.7 jit_solution(1019005398836284077)
XLA Ops:
  0.6 209.7 %shard_map.95.result = f32[5,8,128]{2,1,0:T(8,128)} custom-call(bf16[64,8,8,4,128]{4,3,2,1,0:T(4,128)(2,1)} %bitcast.11, s32[4,4096]{1,0:T(4,128)} %bitcast.14, s32[2,256]{1,0:T(2,128)} %bitcast.16, s32[4,8192]{1,0:T(4,128)} %bitcast.12, f32[4,8192]{1,0:T(4,128)} %bitcast.13, s32[8,8]{1,0:T(8,128)} %bitcast.15, f32[3,8]{1,0:T(4,128)} %bitcast.17, ...), custom_call_target="tpu_custom_call" | custom-call | tf_op jit(solution)/shard_map/pallas_call | solution.py:403
  210.3 1.3 shard_map.96
